TPU v7x, 512 devices: a whole 4x4x16 slice. The times are simulated.
512 devices in a mesh: freq: 64 (over y, z), tm: 2 (over x_lo), bl: 4 (over x_hi, core).
Axes of the slice: x: 4 (x_hi: 2, x_lo: 2; x = x_hi * 2 + x_lo), y: 4, z: 16, core: 2. Of those that a mesh axis runs over, the one named last changes fastest.
Arguments:
- samples: int32 [1024, 128, 2048], P(('freq', 'bl'), 'tm'), may hold values from 0 to 15
- chan_index: int32 [128], replicated, may hold values from 0 to 1023, as said below
Outputs:
- visibilities: float32 [128, 4, 2, 512, 512], P(('freq', 'tm'), 'bl')
Inputs may be any that keep to these rules, and one draw needn't show every extreme that they name: `chan_index`: the entries are distinct.
All inputs are finite; a program needn't handle non-finite values.
Results may differ from a plain program's by a relative error of at most 0.0064.
Values may be sent and summed in bfloat16 or wider, within the bound.
A program may use at most 64 MiB of HBM per device.

v0:
```python
import math

import jax
import jax.numpy as jnp
from jax import lax
from jax.sharding import PartitionSpec as P

TAPS = 4


def from_behind(block, axis, distance):
    devices = range(lax.axis_size(axis))
    route = [(i - distance, i) for i in devices if i - distance in devices]
    return lax.ppermute(block, axis, route)


def tap_table(frame):
    place = jnp.arange(TAPS * frame, dtype=jnp.float32) + 0.5
    shifted = (place - 2.0 * frame) / frame
    window = 0.5 - 0.5 * jnp.cos(place * (2.0 * math.pi / (TAPS * frame)))
    return (jnp.sinc(shifted) * window).reshape(TAPS, frame)


def dft_table(chan_index, frame):
    steps = jnp.arange(frame, dtype=jnp.int32)
    phase = chan_index[None, :] * steps[:, None] % frame
    angle = phase.astype(jnp.float32) * (2.0 * math.pi / frame)
    scale = 1.0 / math.sqrt(frame)
    both = jnp.stack([jnp.cos(angle) * scale, -jnp.sin(angle) * scale], axis=-1)
    return both.reshape(frame, -1).astype(jnp.bfloat16)


def apply_taps(padded, taps):
    count = padded.shape[1] - (TAPS - 1)
    total = taps[0][None, None, :] * padded[:, 0:count]
    for k in range(1, TAPS):
        total = total + taps[k][None, None, :] * padded[:, k : k + count]
    return total


def corner_turn(spectra_t, groups):
    return lax.all_to_all(
        spectra_t.reshape(groups, -1), ("freq", "tm"), split_axis=0, concat_axis=0, tiled=True
    )


def on_device(samples, chan_index):
    in_dev, fr_dev, frame = samples.shape
    chans = chan_index.shape[0]
    n_freq = lax.axis_size("freq")
    n_tm = lax.axis_size("tm")
    n_bl = lax.axis_size("bl")
    groups = n_freq * n_tm
    chan_dev = chans // groups
    taps = tap_table(frame)
    volts = (samples.astype(jnp.float32) - 7.5) * 0.25
    edge = jnp.zeros((in_dev, TAPS - 1, frame), jnp.float32)
    tail = jnp.concatenate([volts[:, fr_dev - (TAPS - 1) :], edge], axis=1)
    carried = apply_taps(tail, taps)
    received = from_behind(carried, "tm", 1)
    own = apply_taps(jnp.concatenate([edge, volts], axis=1), taps)
    filtered = jnp.concatenate([own[:, : TAPS - 1] + received, own[:, TAPS - 1 :]], axis=1)
    filtered = filtered.astype(jnp.bfloat16).reshape(in_dev * fr_dev, frame)
    table = dft_table(chan_index, frame)
    spectra_t = lax.dot_general(
        table, filtered, (((0,), (1,)), ((), ())), preferred_element_type=jnp.float32
    ).astype(jnp.bfloat16)
    moved = corner_turn(spectra_t, groups)
    moved = moved.reshape(n_freq, n_tm, chan_dev, 2, in_dev, fr_dev)
    moved = jnp.transpose(moved, (2, 3, 0, 4, 1, 5))
    mine = moved.reshape(chan_dev, 2, n_freq, in_dev, n_tm * fr_dev)
    gathered = lax.all_gather(mine[None], "bl", axis=0, tiled=True)
    gathered = jnp.transpose(gathered, (1, 2, 3, 0, 4, 5))
    spectra_all = gathered.reshape(chan_dev, 2, n_freq * n_bl * in_dev, n_tm * fr_dev)
    total_in = spectra_all.shape[2]
    frames_all = spectra_all.shape[3]
    half = total_in // 2
    tile = lax.axis_index("bl")
    row_start = tile // 2 * half
    col_start = tile % 2 * half
    rows = lax.dynamic_slice_in_dim(spectra_all, row_start, half, 2)
    cols = lax.dynamic_slice_in_dim(spectra_all, col_start, half, 2)
    right = jnp.concatenate([cols[:, 0], cols[:, 1]], axis=2)
    left_re = jnp.concatenate([rows[:, 0], rows[:, 1]], axis=2)
    left_im = jnp.concatenate([rows[:, 1], -rows[:, 0]], axis=2)
    left = jnp.stack([left_re, left_im], axis=1)
    product = jnp.einsum("cphf,cqf->cphq", left, right, preferred_element_type=jnp.float32)
    return (product / frames_all)[:, None]


def solution(mesh):
    placed = (P(("freq", "bl"), "tm", None), P())
    return jax.shard_map(
        on_device,
        mesh=mesh,
        in_specs=placed,
        out_specs=P(("freq", "tm"), "bl", None, None, None),
        check_vma=False,
    )
```

profile of v0, /device:TPU:1, one launch (start us, length us, event | category | flops | bytes accessed | tf_op | source)
XLA Modules:
  0.0 74.0 jit_solution(4483799580852284554)
XLA Ops:
  0.0 0.2 fusion.27
  0.2 0.0 copy-start
  0.2 2.0 %fusion.6 = f32[4,64,2048]{2,1,0:T(8,128)S(1)} fusion(s32[4,64,2048]{2,1,0:T(8,128)} %param.2), kind=kLoop, calls=%fused_computation.12 | loop fusion | flops 1572864 | bytes 4194304 | tf_op jit(solution)/shard_map/mul | solution.py:56
  2.3 0.1 fusion.20
  2.4 4.0 %collective-permute-start = (f32[4,3,2048]{2,1,0:T(4,128)S(1)}, f32[4,3,2048]{2,1,0:T(4,128)S(1)}, u32[]{:S(2)}, u32[]{:S(2)}) collective-permute-start(f32[4,3,2048]{2,1,0:T(4,128)S(1)} %fusion.20), channel_id=1, source_target_pairs={{0,4},{1,5},{2,6},{3,7},{8,12},{9,13},{10,14},{11,15},{16,20},{17,... | collective-permute-start | bytes 294920 | tf_op jit(solution)/shard_map/ppermute | solution.py:14
  6.3 0.0 copy-done
  6.3 0.0 copy-start.2
  6.3 1.0 %fusion.3 = f32[4,64,2048]{2,1,0:T(8,128)S(1)} fusion(f32[4,64,2048]{2,1,0:T(8,128)S(1)} %fusion.6, s32[4,64,2048]{2,1,0:T(8,128)S(1)} %copy-done, f32[2048]{0:T(1024)S(1)} %get-tuple-element.13, f32[2048]{0:T(1024)S(1)} %get-tuple-element.14, f32[2048]{0:T(1024)S(1)} %get-tuple-element.15, f32[2048]{0:T(1024)S(1)} %get-tuple-element.16), kind=kLoop, calls=%fused_computation.6 | loop fusion | flops 4718592 | bytes 6324224 | tf_op jit(solution)/shard_map/add | solution.py:37
  7.4 0.0 copy-done.2
  7.4 4.4 %multiply_convert_fusion.1 = (bf16[2048,128,1]{1,0,2:T(8,128)(2,1)S(1)}, bf16[2048,128,1]{1,0,2:T(8,128)(2,1)S(1)}) fusion(s32[128]{0:T(128)S(1)} %copy-done.2), kind=kLoop, calls=%fused_computation.23 | loop fusion | flops 4980736 | bytes 1049088 | tf_op jit(solution)/shard_map/convert.3
  11.8 1.1 %pad_maximum_fusion = bf16[2048,128,2]{1,0,2:T(8,128)(2,1)} fusion(bf16[2048,128,1]{1,0,2:T(8,128)(2,1)S(1)} %get-tuple-element.18, bf16[2048,128,1]{1,0,2:T(8,128)(2,1)S(1)} %get-tuple-element.17), kind=kLoop, calls=%fused_computation.20 | loop fusion | flops 524288 | bytes 2097152 | tf_op jit(solution)/shard_map/stack | solution.py:29
  12.9 0.2 slice.129
  13.1 3.7 %copy.14 = bf16[2048,128,2]{0,2,1:T(2,128)(2,1)} copy(bf16[2048,128,2]{1,0,2:T(8,128)(2,1)} %pad_maximum_fusion) | data formatting | bytes 2097152 | tf_op jit(solution)/shard_map/stack | solution.py:29
  16.8 2.2 %convert_element_type.47 = bf16[2048,256]{0,1:T(8,128)(2,1)} reshape(bf16[2048,128,2]{0,2,1:T(2,128)(2,1)} %copy.14) | data formatting | bytes 2097152 | tf_op jit(solution)/shard_map/convert_element_type | solution.py:30
  19.1 0.0 copy-start.1
  19.1 0.0 collective-permute-done
  19.1 0.3 pad_maximum_fusion.1
  19.4 0.9 %copy-done.1 = bf16[2048,256]{0,1:T(8,128)(2,1)S(1)} copy-done((bf16[2048,256]{0,1:T(8,128)(2,1)S(1)}, bf16[2048,256]{0,1:T(8,128)(2,1)}, u32[]{:S(2)}) %copy-start.1) | copy-done | bytes 1048600
  20.3 0.5 convolution_convert_fusion
  20.8 0.1 all_to_all.8
  20.8 0.5 broadcast.161
  21.3 1.4 %reduce.1 = bf16[128,512]{1,0:T(8,128)(2,1)S(1)} reduce(bf16[128,1,512]{2,1,0:T(2,128)(2,1)S(1)} %all_to_all.8, bf16[]{:T(256)} %broadcast.161), dimensions={1}, to_apply=%all_to_all.8.reduce_sub_computation | reduce | bytes 262146 | tf_op jit(solution)/shard_map/all_to_all | solution.py:42
  22.7 0.7 reshape.170
  23.4 19.7 %all-to-all-start = ((bf16[128,2,256]{2,1,0:T(2,128)(2,1)}), bf16[128,2,256]{2,1,0:T(2,128)(2,1)S(1)}, u32[]{:S(2)}, u32[]{:S(2)}) async-start(bf16[128,2,256]{2,1,0:T(2,128)(2,1)} %reshape.170), calls=%async_computation | async-start | bytes 262144 | tf_op jit(solution)/shard_map/all_to_all | solution.py:42
  43.1 15.4 %all-to-all-done = bf16[128,2,256]{2,1,0:T(2,128)(2,1)S(1)} async-done(((bf16[128,2,256]{2,1,0:T(2,128)(2,1)}), bf16[128,2,256]{2,1,0:T(2,128)(2,1)S(1)}, u32[]{:S(2)}, u32[]{:S(2)}) %all-to-all-start) | async-done | bytes 131104 | tf_op jit(solution)/shard_map/all_to_all | solution.py:42
  58.5 0.1 reshape.171
  58.6 0.8 %reduce = bf16[128,512]{1,0:T(8,128)(2,1)S(1)} reduce(bf16[128,1,512]{2,1,0:T(2,128)(2,1)S(1)} %reshape.171, bf16[]{:T(256)} %constant.114), dimensions={1}, to_apply=%all_to_all.7.reduce_sub_computation | reduce | bytes 262146 | tf_op jit(solution)/shard_map/all_to_all | solution.py:42
  59.4 0.2 reshape.164
  59.6 0.2 copy.16
  59.8 0.1 broadcast_in_dim_reshape.3
  60.0 11.7 %all_gather.3 = bf16[4,1,2,64,4,128]{5,3,4,2,1,0:T(8,128)(2,1)S(1)} all-gather(bf16[1,1,2,64,4,128]{5,3,4,2,1,0:T(8,128)(2,1)S(1)} %broadcast_in_dim_reshape.3), channel_id=1, replica_groups=mesh['freq'=64,'tm'=2,'bl'=4] {'bl'}, dimensions={0}, use_global_device_ids=true | all-gather | bytes 655360 | tf_op jit(solution)/shard_map/all_gather | solution.py:72
  71.7 0.4 copy.17
  72.2 0.1 maximum_bitcast_fusion.2
  72.2 1.8 %multiply_bitcast_fusion = f32[1,1,2,512,512]{4,3,2,1,0:T(8,128)} fusion(bf16[1,1,512,256]{3,2,1,0:T(8,128)(2,1)S(1)} %get-tuple-element.11, bf16[1,1,512,256]{3,2,1,0:T(8,128)(2,1)S(1)} %get-tuple-element.10, bf16[1,512,128]{2,1,0:T(8,128)(2,1)S(1)} %get-tuple-element.8, bf16[1,512,128]{2,1,0:T(8,128)(2,1)S(1)} %get-tuple-element.7), kind=kOutput, calls=%fused_computation.10 | convolution fusion | flops 269746176 | bytes 2883584 | tf_op jit(solution)/shard_map/cphf,cqf->cphq/dot_general | solution.py:87
  (5 shorter events, 0.2 us)
Async XLA Ops:
  0.2 6.1 %copy-start = (s32[4,64,2048]{2,1,0:T(8,128)S(1)}, s32[4,64,2048]{2,1,0:T(8,128)}, u32[]{:S(2)}) copy-start(s32[4,64,2048]{2,1,0:T(8,128)} %param.2) | copy-start | bytes 6291460
  2.4 16.7 %collective-permute-start = (f32[4,3,2048]{2,1,0:T(4,128)S(1)}, f32[4,3,2048]{2,1,0:T(4,128)S(1)}, u32[]{:S(2)}, u32[]{:S(2)}) collective-permute-start(f32[4,3,2048]{2,1,0:T(4,128)S(1)} %fusion.20), channel_id=1, source_target_pairs={{0,4},{1,5},{2,6},{3,7},{8,12},{9,13},{10,14},{11,15},{16,20},{17,... | collective-permute-start | bytes 294920 | tf_op jit(solution)/shard_map/ppermute | solution.py:14
  6.3 1.0 %copy-start.2 = (s32[128]{0:T(128)S(1)}, s32[128]{0:T(128)}, u32[]{:S(2)}) copy-start(s32[128]{0:T(128)} %param.3) | copy-start | bytes 1540
  19.1 1.2 %copy-start.1 = (bf16[2048,256]{0,1:T(8,128)(2,1)S(1)}, bf16[2048,256]{0,1:T(8,128)(2,1)}, u32[]{:S(2)}) copy-start(bf16[2048,256]{0,1:T(8,128)(2,1)} %convert_element_type.47) | copy-start | bytes 3145732
  23.4 35.1 %all-to-all-start = ((bf16[128,2,256]{2,1,0:T(2,128)(2,1)}), bf16[128,2,256]{2,1,0:T(2,128)(2,1)S(1)}, u32[]{:S(2)}, u32[]{:S(2)}) async-start(bf16[128,2,256]{2,1,0:T(2,128)(2,1)} %reshape.170), calls=%async_computation | async-start | bytes 262144 | tf_op jit(solution)/shard_map/all_to_all | solution.py:42
where the time goes:
time: 74.3 us; the launch traced here: 74 us
  starting transfers between devices  23.6 us (32%)
  waiting for transfers between devices  15.4 us (21%)
  blocking collectives  11.7 us (16%)
  other arithmetic  11.4 us (15%)
  local copies, waits for them, and re-layouts  9.43 us (13%)
  matrix products  2.25 us (3%)
    all_to_all x1, starting transfers between devices, corner_turn(): lax.all_to_all(spectra_t.reshape(groups, -1), ('freq', 'tm'), split_axis=...  19.7 us
    all_to_all x1, waiting for transfers between devices, corner_turn(): lax.all_to_all(spectra_t.reshape(groups, -1), ('freq', 'tm'), split_axis=...  15.4 us
    all_gather x1, blocking collectives, on_device(): gathered = lax.all_gather(mine[None], 'bl', axis=0, tiled=True)  11.7 us
    another operation x2, other arithmetic  4.46 us
    ppermute x1, starting transfers between devices, from_behind(): return lax.ppermute(block, axis, route)  3.95 us
    another operation x1, local copies, waits for them, and re-layouts, dft_table(): both = jnp.stack([jnp.cos(angle) * scale, -jnp.sin(angle) * scale], axis=-1)  3.71 us
    convert_element_type x1, local copies, waits for them, and re-layouts, dft_table(): return both.reshape(frame, -1).astype(jnp.bfloat16)  2.24 us
    all_to_all x2, other arithmetic, corner_turn(): lax.all_to_all(spectra_t.reshape(groups, -1), ('freq', 'tm'), split_axis=...  2.16 us
  transfers between devices with their start and end apart: 2, of which 1 were waited for; matrix products, arithmetic and copies ran while one was open for 17% of the time, Pallas kernels for 0%

commit v1 on v0

v1 whole, which is shorter than its diff:
```python
import functools
import math

import jax
import jax.numpy as jnp
import numpy as np
from jax import lax
from jax.experimental import pallas as pl
from jax.experimental.pallas import tpu as pltpu
from jax.sharding import PartitionSpec as P

TAPS = 4
FRAME = 2048
NY, NZ, NX = 4, 16, 2
CHANS = NY * NZ * NX
LANES = 128
MESH = pl.DeviceIdType.MESH
OFFSETS = (0, 1, -1, 2, -2, 3, -3, 4, -4, 5, -5, 6, -6, 7, -7, 8)
WAVES = ((0, 8), (8, 16))


def tap_constants():
    place = np.arange(TAPS * FRAME, dtype=np.float64) + 0.5
    shifted = (place - 2.0 * FRAME) / FRAME
    window = 0.5 - 0.5 * np.cos(place * (2.0 * math.pi / (TAPS * FRAME)))
    return (np.sinc(shifted) * window).reshape(TAPS, FRAME).astype(np.float32)


def cos_sin(phase):
    quarter = FRAME // 4
    turn = (phase + quarter // 2) // quarter
    rest = (phase - turn * quarter).astype(jnp.float32) * (2.0 * math.pi / FRAME)
    sq = rest * rest
    sin = rest * (1.0 + sq * (-1.0 / 6 + sq * (1.0 / 120 + sq * (-1.0 / 5040 + sq * (1.0 / 362880)))))
    cos = 1.0 + sq * (-0.5 + sq * (1.0 / 24 + sq * (-1.0 / 720 + sq * (1.0 / 40320))))
    odd = turn % 2 == 1
    c = jnp.where(odd, sin, cos)
    s = jnp.where(odd, cos, sin)
    c = jnp.where((turn % 4 == 1) | (turn % 4 == 2), -c, c)
    s = jnp.where(turn % 4 >= 2, -s, s)
    return c, s


def taps_applied(ext, taps):
    prior = pltpu.roll(ext, 1, 0)
    early = taps[1:2] * ext + taps[0:1] * prior
    late = taps[3:4] * ext + taps[2:3] * prior
    return (late + pltpu.roll(early, 2, 0))[8:].astype(jnp.bfloat16)


def to_volts(samples):
    return (samples.astype(jnp.float32) - 7.5) * 0.25


def channelize_kernel(
    samples, chan_ref, taps_ref, turned,
    raw, filtered, table, spread, mine, held, edge_out, edge_in,
    load_sem, edge_sem, zsend, zrecv, psend, own_sem, precv,
):
    freq = lax.axis_index("freq")
    tm = lax.axis_index("tm")
    bl = lax.axis_index("bl")
    y, z = freq // NZ, freq % NZ
    half = y // 2

    loads = [pltpu.make_async_copy(samples.at[:, 56:64], raw.at[:, 56:64], load_sem.at[0])]
    for i in range(4):
        loads.append(pltpu.make_async_copy(samples.at[i, 0:56], raw.at[i, 0:56], load_sem.at[1 + i]))
    for copy in loads:
        copy.start()

    barrier = pltpu.get_barrier_semaphore()
    for d in range(1, NZ):
        pl.semaphore_signal(barrier, inc=1, device_id=(y * NZ + (z + d) % NZ, tm, bl), device_id_type=MESH)
    for n in range(1, 32):
        yo, xo, bo = n // 8, n // 4 % 2, n % 4
        peer = ((y + yo) % NY * NZ + z, (tm + xo) % NX, (bl + bo) % 4)
        pl.semaphore_signal(barrier, inc=1, device_id=peer, device_id_type=MESH)

    row = lax.broadcasted_iota(jnp.int32, (CHANS, LANES), 0)
    lane = lax.broadcasted_iota(jnp.int32, (CHANS, LANES), 1)
    source = (row // 2 % NY) * (NZ * NX) + row // 8 * NX + row % 2
    picked = jnp.where(lane == source, jnp.broadcast_to(chan_ref[...], (CHANS, LANES)), 0)
    chan = jnp.broadcast_to(jnp.sum(picked.astype(jnp.float32), axis=1, keepdims=True), (CHANS, LANES))
    chan = chan.astype(jnp.int32)
    scale = 1.0 / math.sqrt(FRAME)
    re, im = cos_sin(chan * lane % FRAME)
    parts = [(re * scale, -im * scale)]
    for step in (128, 256, 512, 1024):
        c, s = cos_sin(chan * step % FRAME)
        parts += [(a * c + b * s, b * c - a * s) for a, b in parts]
    for k, (a, b) in enumerate(parts):
        table[0:CHANS, k * LANES : (k + 1) * LANES] = a.astype(jnp.bfloat16)
        table[CHANS:, k * LANES : (k + 1) * LANES] = b.astype(jnp.bfloat16)

    loads[0].wait()
    edge_copy = pltpu.make_async_remote_copy(
        edge_out, edge_in, edge_sem.at[0], edge_sem.at[1],
        device_id=(freq, 1 - tm, bl), device_id_type=MESH,
    )
    for i in range(4):
        edge_out[4 * i : 4 * i + 4] = to_volts(raw[i, 60:64]).astype(jnp.bfloat16)
    pl.semaphore_wait(barrier, 46)

    @pl.when(tm == 0)
    def _():
        edge_copy.start()

    for i in range(4):
        loads[1 + i].wait()

        @pl.loop(0, FRAME // LANES)
        def _(k):
            cols = pl.ds(pl.multiple_of(k * LANES, LANES), LANES)
            filtered[i * 64 + 8 : i * 64 + 64, cols] = taps_applied(to_volts(raw[i, :, cols]), taps_ref[:, cols])

    @pl.when(tm == 0)
    def _():
        edge_in[...] = jnp.zeros_like(edge_in)
        edge_copy.wait_send()

    @pl.when(tm == 1)
    def _():
        edge_copy.wait_recv()

    @pl.loop(0, FRAME // LANES)
    def _(k):
        cols = pl.ds(pl.multiple_of(k * LANES, LANES), LANES)
        before = edge_in[:, cols].astype(jnp.float32)
        for i in range(4):
            ext = jnp.concatenate(
                [before[4 * i : 4 * i + 4], before[4 * i : 4 * i + 4], to_volts(raw[i, 0:8, cols])], axis=0
            )
            filtered[i * 64 : i * 64 + 8, cols] = taps_applied(ext, taps_ref[:, cols])

    spectra = lax.dot_general(
        table[...], filtered[...], (((1,), (1,)), ((), ())), preferred_element_type=jnp.float32
    )
    first = lane < 64
    for t in range(2):
        re = spectra[:CHANS, t * LANES : (t + 1) * LANES]
        im = spectra[CHANS:, t * LANES : (t + 1) * LANES]
        spread[pl.ds(2 * t, CHANS, stride=4), :] = jnp.where(first, re, pltpu.roll(im, 64, 1))
        spread[pl.ds(2 * t + 1, CHANS, stride=4), :] = jnp.where(first, pltpu.roll(re, 64, 1), im)
    mine[...] = spread[...].astype(jnp.bfloat16).reshape(NZ, NY * NX, 4, LANES)

    own = pltpu.make_async_copy(mine.at[z], held.at[0], zrecv.at[0])
    own.start()
    for slot in range(1, NZ):
        to = (z - OFFSETS[slot] + NZ) % NZ
        pltpu.make_async_remote_copy(
            mine.at[to], held.at[slot], zsend, zrecv.at[0 if slot < 8 else 1],
            device_id=(y * NZ + to, tm, bl), device_id_type=MESH,
        ).start()

    for w, (lo, hi) in enumerate(WAVES):
        pltpu.make_async_copy(held.at[lo:hi], held.at[lo:hi], zrecv.at[w]).wait()
        land = turned.at[tm, y, lo:hi, bl]
        for yo in range(NY):
            for xo in range(NX):
                y_to, x_to = (y + yo) % NY, (tm + xo) % NX
                block = held.at[lo:hi, y_to * NX + x_to]
                for j, to in enumerate((1, 2, 3 * half)):
                    remote = yo or xo
                    copy = pltpu.make_async_remote_copy(
                        block, land, psend.at[w] if remote else own_sem.at[w, j], precv.at[w],
                        device_id=(y_to * NZ + z, x_to, to), device_id_type=MESH,
                    )
                    if remote:
                        copy.start()
                        continue

                    @pl.when(to != bl)
                    def _():
                        copy.start()

                    @pl.when(to == bl)
                    def _():
                        pltpu.make_async_copy(block, land, precv.at[w]).start()

    for w, (lo, hi) in enumerate(WAVES):
        sent = spread.at[0 : 42 * (hi - lo)]
        pltpu.make_async_copy(sent, sent, psend.at[w]).wait()
        block = held.at[lo:hi, 0]
        for j, to in enumerate((1, 2, 3 * half)):

            @pl.when(to != bl)
            def _():
                pltpu.make_async_copy(block, block, own_sem.at[w, j]).wait()

        middle = (bl == 1) | (bl == 2)

        @pl.when(middle)
        def _():
            got = turned.at[:, :, lo:hi]
            pltpu.make_async_copy(got, got, precv.at[w]).wait()

        @pl.when(jnp.logical_not(middle))
        def _():
            got = turned.at[:, 0:2, lo:hi]
            pltpu.make_async_copy(got, got, precv.at[w]).wait()

    sent = mine.at[0 : NZ - 1]
    pltpu.make_async_copy(sent, sent, zsend).wait()


def correlate_kernel(turned, out, rows, turned_rows, cols):
    z = lax.axis_index("freq") % NZ
    bl = lax.axis_index("bl")
    sign = jnp.where(lax.broadcasted_iota(jnp.int32, (16, LANES), 1) < 64, 1.0, -1.0)

    @pl.when(pl.program_id(0) == 0)
    def _():
        for slot in range(NZ):
            at = (z + OFFSETS[slot] + NZ) % NZ * 16
            for yi in range(2):
                place = pl.ds(pl.multiple_of(at + yi * 256, 16), 16)
                for x in range(NX):
                    k = slice(x * LANES, (x + 1) * LANES)
                    block = turned[x, bl // 2 * 2 + yi, slot]
                    rows[place, k] = block
                    turned_rows[place, k] = (pltpu.roll(block.astype(jnp.float32), 64, 1) * sign).astype(jnp.bfloat16)
                    cols[place, k] = turned[x, bl % 2 * 2 + yi, slot]

    count = out.shape[3]
    part = pl.ds(pl.multiple_of(pl.program_id(0) * count, count), count)
    for p, left in enumerate((rows, turned_rows)):
        product = lax.dot_general(
            left[part], cols[...], (((1,), (1,)), ((), ())), preferred_element_type=jnp.float32
        )
        out[0, 0, p] = product * (1.0 / 128)


def on_device(samples, chan_index):
    bf16, f32 = jnp.bfloat16, jnp.float32
    vmem = pl.BlockSpec(memory_space=pltpu.VMEM)
    anywhere = pl.BlockSpec(memory_space=pl.ANY)
    dma = pltpu.SemaphoreType.DMA
    turned = pl.pallas_call(
        channelize_kernel,
        out_shape=jax.ShapeDtypeStruct((NX, NY, NZ, 4, 4, LANES), bf16),
        in_specs=[anywhere, vmem, vmem],
        out_specs=anywhere,
        scratch_shapes=[
            pltpu.VMEM((4, 64, FRAME), jnp.int32),
            pltpu.VMEM((256, FRAME), bf16),
            pltpu.VMEM((2 * CHANS, FRAME), bf16),
            pltpu.VMEM((4 * CHANS, LANES), f32),
            pltpu.VMEM((NZ, NY * NX, 4, LANES), bf16),
            pltpu.VMEM((NZ, NY * NX, 4, LANES), bf16),
            pltpu.VMEM((16, FRAME), bf16),
            pltpu.VMEM((16, FRAME), bf16),
            dma((5,)),
            dma((2,)),
            dma,
            dma((2,)),
            dma((2,)),
            dma((2, 3)),
            dma((2,)),
        ],
        compiler_params=pltpu.CompilerParams(
            collective_id=0, has_side_effects=True, vmem_limit_bytes=40 * 2**20
        ),
        name="channelize",
    )(samples, chan_index.reshape(1, CHANS), jnp.asarray(tap_constants()))
    turned = turned.reshape(NX, NY, NZ, 16, LANES)
    steps = 4
    return pl.pallas_call(
        correlate_kernel,
        out_shape=jax.ShapeDtypeStruct((1, 1, 2, 512, 512), f32),
        grid=(steps,),
        in_specs=[vmem],
        out_specs=pl.BlockSpec((1, 1, 2, 512 // steps, 512), lambda i: (0, 0, 0, i, 0)),
        scratch_shapes=[pltpu.VMEM((512, 256), bf16)] * 3,
        compiler_params=pltpu.CompilerParams(vmem_limit_bytes=40 * 2**20),
        name="correlate",
    )(turned)


def solution(mesh):
    placed = (P(("freq", "bl"), "tm", None), P())
    return jax.shard_map(
        on_device,
        mesh=mesh,
        in_specs=placed,
        out_specs=P(("freq", "tm"), "bl", None, None, None),
        check_vma=False,
    )
```

time: 74.3 us -> 42.7 us (0.57)
  Pallas kernels: 0 us -> 39.4 us
  starting transfers between devices: 23.6 us -> 0 us
  waiting for transfers between devices: 15.4 us -> 0 us
  blocking collectives: 11.7 us -> 0 us
  other arithmetic: 11.4 us -> 0 us
  local copies, waits for them, and re-layouts: 9.43 us -> 3 us
  matrix products: 2.25 us -> 0 us
    pallas_call x0 -> x2, Pallas kernels: none -> 39.4 us  [the longest x1 36.7 us: on_device(): pl.pallas_call(channelize_kernel, out_shape=jax.ShapeDtypeStruct((NX, NY,...]
    all_to_all x1 -> x0, starting transfers between devices: 19.7 us -> none  [corner_turn(): lax.all_to_all(spectra_t.reshape(groups, -1), ('freq', 'tm'), split_axis=...]
    all_to_all x1 -> x0, waiting for transfers between devices: 15.4 us -> none  [corner_turn(): lax.all_to_all(spectra_t.reshape(groups, -1), ('freq', 'tm'), split_axis=...]
    all_gather x1 -> x0, blocking collectives: 11.7 us -> none  [on_device(): gathered = lax.all_gather(mine[None], 'bl', axis=0, tiled=True)]
    another operation x4 -> x0, other arithmetic: 5.58 us -> none
    ppermute x1 -> x0, starting transfers between devices: 3.95 us -> none  [from_behind(): return lax.ppermute(block, axis, route)]
    another operation x2 -> x0, local copies, waits for them, and re-layouts: 3.86 us -> none  [the longest x1 3.71 us: dft_table(): both = jnp.stack([jnp.cos(angle) * scale, -jnp.sin(angle) * scale], axis=-1)]
    dot_general x2 -> x0, matrix products: 2.25 us -> none  [the longest x1 1.79 us: on_device(): jnp.einsum('cphf,cqf->cphq', left, right, preferred_element_type=jnp.floa...]
  transfers between devices with their start and end apart: 2 -> 0, of which waited for: 1 -> 0; matrix products, arithmetic and copies ran while one was open for 17% -> 0% of each run, Pallas kernels for 0% -> 0%
where the time goes in v1:
time: 42.7 us; the launch traced here: 42.4 us
  Pallas kernels  39.4 us (92%)
  local copies, waits for them, and re-layouts  3 us (7%)
    pallas_call x1, Pallas kernels, on_device(): pl.pallas_call(channelize_kernel, out_shape=jax.ShapeDtypeStruct((NX, NY,...  36.7 us
    unnamed x6, local copies, waits for them, and re-layouts  3 us
    pallas_call x1, Pallas kernels, on_device(): pl.pallas_call(correlate_kernel, out_shape=jax.ShapeDtypeStruct((1, 1, 2,...  2.77 us

profile of v1, /device:TPU:1, one launch (start us, length us, event | category | flops | bytes accessed | tf_op | source)
XLA Modules:
  0.0 42.4 jit_solution(10288363133545729987)
XLA Ops:
  0.0 0.0 copy-start
  0.0 1.6 %copy-done = s32[4,64,2048]{2,1,0:T(8,128)S(1)} copy-done((s32[4,64,2048]{2,1,0:T(8,128)S(1)}, s32[4,64,2048]{2,1,0:T(8,128)}, u32[]{:S(2)}) %copy-start) | copy-done | bytes 2097176
  1.6 0.0 copy-start.1
  1.6 0.8 %copy-done.1 = f32[4,2048]{1,0:T(4,128)S(1)} copy-done((f32[4,2048]{1,0:T(4,128)S(1)}, f32[4,2048]{1,0:T(4,128)}, u32[]{:S(2)}) %copy-start.1) | copy-done | bytes 32792
  2.4 0.0 copy-start.2
  2.4 0.7 %copy-done.2 = s32[128]{0:T(128)S(1)} copy-done((s32[128]{0:T(128)S(1)}, s32[128]{0:T(128)}, u32[]{:S(2)}) %copy-start.2) | copy-done | bytes 536
  3.0 36.7 %channelize.1 = bf16[2,4,16,4,4,128]{5,4,3,2,1,0:T(4,128)(2,1)S(1)} custom-call(s32[4,64,2048]{2,1,0:T(8,128)S(1)} %copy-done, s32[1,128]{1,0:T(1,128)S(1)} %bitcast.3, f32[4,2048]{1,0:T(4,128)S(1)} %copy-done.1), custom_call_target="tpu_custom_call" | custom-call | tf_op jit(solution)/shard_map/channelize/pallas_call | solution.py:239
  39.7 2.8 %correlate.1 = f32[1,1,2,512,512]{4,3,2,1,0:T(8,128)} custom-call(bf16[2,4,16,16,128]{4,3,2,1,0:T(8,128)(2,1)S(1)} %bitcast.2), custom_call_target="tpu_custom_call" | custom-call | tf_op jit(solution)/shard_map/correlate/pallas_call | solution.py:268
Async XLA Ops:
  0.0 1.6 %copy-start = (s32[4,64,2048]{2,1,0:T(8,128)S(1)}, s32[4,64,2048]{2,1,0:T(8,128)}, u32[]{:S(2)}) copy-start(s32[4,64,2048]{2,1,0:T(8,128)} %samples.1) | copy-start | bytes 6291460
  1.6 0.8 %copy-start.1 = (f32[4,2048]{1,0:T(4,128)S(1)}, f32[4,2048]{1,0:T(4,128)}, u32[]{:S(2)}) copy-start(f32[4,2048]{1,0:T(4,128)} %constant.2.clone.taps_ref) | copy-start | bytes 98308
  2.4 0.7 %copy-start.2 = (s32[128]{0:T(128)S(1)}, s32[128]{0:T(128)}, u32[]{:S(2)}) copy-start(s32[128]{0:T(128)} %param.4) | copy-start | bytes 1540

commit v2 on v1

v2 whole, which is shorter than its diff:
```python
import math

import jax
import jax.numpy as jnp
import numpy as np
from jax import lax
from jax.experimental import pallas as pl
from jax.experimental.pallas import tpu as pltpu
from jax.sharding import PartitionSpec as P

TAPS = 4
FRAME = 2048
NY, NZ, NX = 4, 16, 2
CHANS = NY * NZ * NX
LANES = 128
MESH = pl.DeviceIdType.MESH
WAVES = ((0, 8), (8, 16))
VMEM_LIMIT = 58 * 2**20
STEPS = 4


def tap_constants():
    place = np.arange(TAPS * FRAME, dtype=np.float64) + 0.5
    shifted = (place - 2.0 * FRAME) / FRAME
    window = 0.5 - 0.5 * np.cos(place * (2.0 * math.pi / (TAPS * FRAME)))
    return (np.sinc(shifted) * window).reshape(TAPS, FRAME).astype(np.float32)


def cos_sin(phase):
    turn = (phase + FRAME // 8) >> 9
    rest = (phase - (turn << 9)).astype(jnp.float32) * (2.0 * math.pi / FRAME)
    sq = rest * rest
    sin = rest * (1.0 + sq * (-1.0 / 6 + sq * (1.0 / 120 + sq * (-1.0 / 5040 + sq * (1.0 / 362880)))))
    cos = 1.0 + sq * (-0.5 + sq * (1.0 / 24 + sq * (-1.0 / 720 + sq * (1.0 / 40320))))
    odd = (turn & 1) == 1
    c = jnp.where(odd, sin, cos)
    s = jnp.where(odd, cos, sin)
    c = jnp.where(((turn + 1) & 2) == 2, -c, c)
    s = jnp.where((turn & 2) == 2, -s, s)
    return c, s


def taps_applied(ext, taps):
    prior = pltpu.roll(ext, 1, 0)
    early = taps[1:2] * ext + taps[0:1] * prior
    late = taps[3:4] * ext + taps[2:3] * prior
    return (late + pltpu.roll(early, 2, 0))[8:].astype(jnp.bfloat16)


def to_volts(samples):
    return (samples.astype(jnp.float32) - 7.5) * 0.25


def make_table(chan_ref, table):
    rows = 16
    lane = lax.broadcasted_iota(jnp.int32, (rows, LANES), 1)
    scale = 1.0 / math.sqrt(FRAME)

    @pl.loop(0, CHANS // rows)
    def _(block):
        row = lax.broadcasted_iota(jnp.int32, (rows, LANES), 0) + block * rows
        source = ((row >> 1) & 3) * (NZ * NX) + (row >> 3) * NX + (row & 1)
        picked = jnp.where(lane == source, jnp.broadcast_to(chan_ref[...], (rows, LANES)), 0)
        chan = jnp.sum(picked.astype(jnp.float32), axis=1, keepdims=True)
        chan = jnp.broadcast_to(chan, (rows, LANES)).astype(jnp.int32)
        re, im = cos_sin((chan * lane) & (FRAME - 1))
        parts = [(re * scale, -im * scale)]
        for step in (128, 256):
            c, s = cos_sin((chan * step) & (FRAME - 1))
            parts += [(a * c + b * s, b * c - a * s) for a, b in parts]
        quarter = chan & 3
        c = jnp.where(quarter == 0, 1.0, jnp.where(quarter == 2, -1.0, 0.0))
        s = jnp.where(quarter == 1, 1.0, jnp.where(quarter == 3, -1.0, 0.0))
        parts += [(a * c + b * s, b * c - a * s) for a, b in parts]
        sign = (1 - 2 * (chan & 1)).astype(jnp.float32)
        parts += [(a * sign, b * sign) for a, b in parts]
        at = pl.multiple_of(block * rows, rows)
        for k, (a, b) in enumerate(parts):
            table[pl.ds(at, rows), k * LANES : (k + 1) * LANES] = a.astype(jnp.bfloat16)
            table[pl.ds(at + CHANS, rows), k * LANES : (k + 1) * LANES] = b.astype(jnp.bfloat16)


def channelize_kernel(
    samples, chan_hbm, taps_hbm, turned,
    raw, chan_ref, taps_ref, filtered, table, spread, mine, held, edge_out, edge_in,
    load_sem, edge_sem, zsend, zrecv, psend, own_sem, precv, in_sem, plane_sem,
):
    freq = lax.axis_index("freq")
    tm = lax.axis_index("tm")
    bl = lax.axis_index("bl")
    y, z = freq // NZ, freq % NZ
    half = y // 2

    loads = [
        pltpu.make_async_copy(chan_hbm, chan_ref, load_sem.at[5]),
        pltpu.make_async_copy(samples.at[:, 56:64], raw.at[:, 56:64], load_sem.at[0]),
        pltpu.make_async_copy(taps_hbm, taps_ref, load_sem.at[6]),
    ]
    for i in range(4):
        loads.append(pltpu.make_async_copy(samples.at[i, 0:56], raw.at[i, 0:56], load_sem.at[1 + i]))
    for copy in loads:
        copy.start()

    barrier = pltpu.get_barrier_semaphore()
    partner = (freq, 1 - tm, bl)

    @pl.when(tm == 1)
    def _():
        pl.semaphore_signal(barrier, inc=1, device_id=partner, device_id_type=MESH)

    @pl.loop(z + 1, NZ)
    def _(t):
        pl.semaphore_signal(barrier, inc=1, device_id=(y * NZ + t, tm, bl), device_id_type=MESH)

    for n in range(15, -1, -1):
        peer = ((y + n // 4) % NY * NZ + z, 1, (bl + n) % 4)
        if n:
            pl.semaphore_signal(barrier, inc=1, device_id=peer, device_id_type=MESH)
            continue

        @pl.when(tm == 0)
        def _():
            pl.semaphore_signal(barrier, inc=1, device_id=peer, device_id_type=MESH)

    loads[0].wait()
    make_table(chan_ref, table)

    loads[1].wait()
    edge_copy = pltpu.make_async_remote_copy(
        edge_out, edge_in, edge_sem.at[0], edge_sem.at[1], device_id=partner, device_id_type=MESH
    )
    for i in range(4):
        edge_out[4 * i : 4 * i + 4] = to_volts(raw[i, 60:64]).astype(jnp.bfloat16)
    loads[2].wait()

    @pl.when(tm == 0)
    def _():
        pl.semaphore_wait(barrier, z + 1)
        edge_copy.start()

    for i in range(4):
        loads[3 + i].wait()

        @pl.loop(0, FRAME // LANES)
        def _(k):
            cols = pl.ds(pl.multiple_of(k * LANES, LANES), LANES)
            filtered[i * 64 + 8 : i * 64 + 64, cols] = taps_applied(to_volts(raw[i, :, cols]), taps_ref[:, cols])

    @pl.when(tm == 0)
    def _():
        edge_in[...] = jnp.zeros_like(edge_in)
        edge_copy.wait_send()

    @pl.when(tm == 1)
    def _():
        pl.semaphore_wait(barrier, z + 31)
        pl.semaphore_signal(plane_sem, inc=1, device_id=partner, device_id_type=MESH)
        edge_copy.wait_recv()

    @pl.loop(0, z)
    def _(t):
        pl.semaphore_signal(in_sem.at[z], inc=1, device_id=(y * NZ + t, tm, bl), device_id_type=MESH)

    @pl.loop(0, FRAME // LANES)
    def _(k):
        cols = pl.ds(pl.multiple_of(k * LANES, LANES), LANES)
        before = edge_in[:, cols].astype(jnp.float32)
        for i in range(4):
            ext = jnp.concatenate(
                [before[4 * i : 4 * i + 4], before[4 * i : 4 * i + 4], to_volts(raw[i, 0:8, cols])], axis=0
            )
            filtered[i * 64 : i * 64 + 8, cols] = taps_applied(ext, taps_ref[:, cols])

    spectra = lax.dot_general(
        table[...], filtered[...], (((1,), (1,)), ((), ())), preferred_element_type=jnp.float32
    )
    first = lax.broadcasted_iota(jnp.int32, (CHANS, LANES), 1) < 64
    for t in range(2):
        re = spectra[:CHANS, t * LANES : (t + 1) * LANES]
        im = spectra[CHANS:, t * LANES : (t + 1) * LANES]
        spread[pl.ds(2 * t, CHANS, stride=4), :] = jnp.where(first, re, pltpu.roll(im, 64, 1))
        spread[pl.ds(2 * t + 1, CHANS, stride=4), :] = jnp.where(first, pltpu.roll(re, 64, 1), im)
    mine[...] = spread[...].astype(jnp.bfloat16).reshape(NZ, NY * NX, 4, LANES)

    wave = z // 8

    def send_along(t):
        pltpu.make_async_remote_copy(
            mine.at[t], held.at[z], zsend, zrecv.at[wave],
            device_id=(y * NZ + t, tm, bl), device_id_type=MESH,
        ).start()

    @pl.loop(0, z)
    def _(t):
        send_along(t)

    pltpu.make_async_copy(mine.at[z], held.at[z], zrecv.at[wave]).start()

    @pl.loop(z + 1, NZ)
    def _(t):
        pl.semaphore_wait(in_sem.at[t], 1)
        send_along(t)

    @pl.when(tm == 0)
    def _():
        pl.semaphore_wait(plane_sem, 1)

    for w, (lo, hi) in enumerate(WAVES):
        pltpu.make_async_copy(held.at[lo:hi], held.at[lo:hi], zrecv.at[w]).wait()
        land = turned.at[tm, y, lo:hi, bl]
        for yo in (2, 1, 3, 0):
            for xo in (1, 0):
                y_to, x_to = (y + yo) % NY, (tm + xo) % NX
                block = held.at[lo:hi, y_to * NX + x_to]
                for j, to in enumerate((1, 2, 3 * half)):
                    remote = yo or xo
                    copy = pltpu.make_async_remote_copy(
                        block, land, psend.at[w] if remote else own_sem.at[w, j], precv.at[w],
                        device_id=(y_to * NZ + z, x_to, to), device_id_type=MESH,
                    )
                    if remote:
                        copy.start()
                        continue

                    @pl.when(to != bl)
                    def _():
                        copy.start()

                    @pl.when(to == bl)
                    def _():
                        pltpu.make_async_copy(block, land, precv.at[w]).start()

    for w, (lo, hi) in enumerate(WAVES):
        sent = spread.at[0 : 42 * (hi - lo)]
        pltpu.make_async_copy(sent, sent, psend.at[w]).wait()
        block = held.at[lo:hi, 0]
        for j, to in enumerate((1, 2, 3 * half)):

            @pl.when(to != bl)
            def _():
                pltpu.make_async_copy(block, block, own_sem.at[w, j]).wait()

        middle = (bl == 1) | (bl == 2)

        @pl.when(middle)
        def _():
            got = turned.at[:, :, lo:hi]
            pltpu.make_async_copy(got, got, precv.at[w]).wait()

        @pl.when(jnp.logical_not(middle))
        def _():
            got = turned.at[:, 0:2, lo:hi]
            pltpu.make_async_copy(got, got, precv.at[w]).wait()

    sent = mine.at[0 : NZ - 1]
    pltpu.make_async_copy(sent, sent, zsend).wait()


def correlate_kernel(turned_hbm, out, turned, made, load_sem, sems):
    bl = lax.axis_index("bl")
    load = pltpu.make_async_copy(turned_hbm, turned, load_sem)
    load.start()
    load.wait()
    sign = jnp.where(lax.broadcasted_iota(jnp.int32, (1, LANES), 1) < 64, 1.0, -1.0)
    right = pl.ds(pl.multiple_of(bl % 2 * 512, 512), 512)
    cols = jnp.concatenate([turned[0, right], turned[1, right]], axis=1)
    count = 512 // STEPS
    copies = []
    for step in range(STEPS):
        part = pl.ds(pl.multiple_of(bl // 2 * 512 + step * count, count), count)
        halves = [turned[x, part] for x in range(NX)]
        turned_halves = [(pltpu.roll(h.astype(jnp.float32), 64, 1) * sign).astype(jnp.bfloat16) for h in halves]
        left = jnp.concatenate([jnp.concatenate(h, axis=1) for h in (halves, turned_halves)], axis=0)
        product = lax.dot_general(left, cols, (((1,), (1,)), ((), ())), preferred_element_type=jnp.float32)
        place = slice(step * count, (step + 1) * count)
        for p in range(2):
            made[0, 0, p, place] = product[p * count : (p + 1) * count] * (1.0 / 128)
        copies.append(pltpu.make_async_copy(made.at[:, :, :, place], out.at[:, :, :, place], sems.at[step]))
        copies[-1].start()
    for copy in copies:
        copy.wait()


def on_device(samples, chan_index):
    bf16, f32 = jnp.bfloat16, jnp.float32
    hbm = pl.BlockSpec(memory_space=pltpu.MemorySpace.HBM)
    dma = pltpu.SemaphoreType.DMA
    turned = pl.pallas_call(
        channelize_kernel,
        out_shape=jax.ShapeDtypeStruct((NX, NY, NZ, 4, 4, LANES), bf16),
        in_specs=[hbm, hbm, hbm],
        out_specs=pl.BlockSpec(memory_space=pl.ANY),
        scratch_shapes=[
            pltpu.VMEM((4, 64, FRAME), jnp.int32),
            pltpu.VMEM((1, CHANS), jnp.int32),
            pltpu.VMEM((TAPS, FRAME), f32),
            pltpu.VMEM((256, FRAME), bf16),
            pltpu.VMEM((2 * CHANS, FRAME), bf16),
            pltpu.VMEM((4 * CHANS, LANES), f32),
            pltpu.VMEM((NZ, NY * NX, 4, LANES), bf16),
            pltpu.VMEM((NZ, NY * NX, 4, LANES), bf16),
            pltpu.VMEM((16, FRAME), bf16),
            pltpu.VMEM((16, FRAME), bf16),
            dma((7,)),
            dma((2,)),
            dma,
            dma((2,)),
            dma((2,)),
            dma((2, 3)),
            dma((2,)),
            pltpu.SemaphoreType.REGULAR((NZ,)),
            pltpu.SemaphoreType.REGULAR,
        ],
        compiler_params=pltpu.CompilerParams(
            collective_id=0, has_side_effects=True, vmem_limit_bytes=VMEM_LIMIT
        ),
        name="channelize",
    )(samples, chan_index.reshape(1, CHANS), jnp.asarray(tap_constants()))
    turned = turned.reshape(NX, NY * NZ * 16, LANES)
    return pl.pallas_call(
        correlate_kernel,
        out_shape=jax.ShapeDtypeStruct((1, 1, 2, 512, 512), f32),
        in_specs=[hbm],
        out_specs=hbm,
        scratch_shapes=[
            pltpu.VMEM((NX, NY * NZ * 16, LANES), bf16),
            pltpu.VMEM((1, 1, 2, 512, 512), f32),
            dma,
            dma((STEPS,)),
        ],
        compiler_params=pltpu.CompilerParams(vmem_limit_bytes=VMEM_LIMIT),
        name="correlate",
    )(turned)


def solution(mesh):
    placed = (P(("freq", "bl"), "tm", None), P())
    return jax.shard_map(
        on_device,
        mesh=mesh,
        in_specs=placed,
        out_specs=P(("freq", "tm"), "bl", None, None, None),
        check_vma=False,
    )
```

time: 42.7 us -> 33.9 us (0.79)
  Pallas kernels: 39.4 us -> 33.7 us
  local copies, waits for them, and re-layouts: 3 us -> 0 us
    pallas_call x1, Pallas kernels: 36.7 us -> 31 us  [on_device(): pl.pallas_call(channelize_kernel, out_shape=jax.ShapeDtypeStruct((NX, NY,...]
    unnamed x6 -> x0, local copies, waits for them, and re-layouts: 3 us -> none
where the time goes in v2:
time: 33.9 us; the launch traced here: 33.7 us
  Pallas kernels  33.7 us (99%)
    pallas_call x1, Pallas kernels, on_device(): pl.pallas_call(channelize_kernel, out_shape=jax.ShapeDtypeStruct((NX, NY,...  31 us
    pallas_call x1, Pallas kernels, on_device(): pl.pallas_call(correlate_kernel, out_shape=jax.ShapeDtypeStruct((1, 1, 2,...  2.67 us

profile of v2, /device:TPU:1, one launch (start us, length us, event | category | flops | bytes accessed | tf_op | source)
XLA Modules:
  0.0 33.7 jit_solution(2751292085627726650)
XLA Ops:
  0.0 31.0 %channelize.1 = bf16[2,4,16,4,4,128]{5,4,3,2,1,0:T(4,128)(2,1)} custom-call(s32[4,64,2048]{2,1,0:T(8,128)} %samples.1, s32[1,128]{1,0:T(1,128)} %bitcast.3, f32[4,2048]{1,0:T(4,128)} %constant.2.clone.taps_hbm), custom_call_target="tpu_custom_call" | custom-call | tf_op jit(solution)/shard_map/channelize/pallas_call | solution.py:288
  31.0 2.7 %correlate.1 = f32[1,1,2,512,512]{4,3,2,1,0:T(8,128)} custom-call(bf16[2,1024,128]{2,1,0:T(8,128)(2,1)} %bitcast.2), custom_call_target="tpu_custom_call" | custom-call | tf_op jit(solution)/shard_map/correlate/pallas_call | solution.py:320

commit v3 on v2

v3 whole, which is shorter than its diff:
```python
import math

import jax
import jax.numpy as jnp
import numpy as np
from jax import lax
from jax.experimental import pallas as pl
from jax.experimental.pallas import tpu as pltpu
from jax.sharding import PartitionSpec as P

TAPS = 4
FRAME = 2048
NY, NZ, NX = 4, 16, 2
CHANS = NY * NZ * NX
LANES = 128
MESH = pl.DeviceIdType.MESH
OFFSETS = (0, 1, -1, 2, -2, 3, -3, 4, -4, 5, -5, 6, -6, 7, -7, 8)
WAVES = ((0, 7), (7, 11), (11, 15), (15, 16))
EARLY = NZ // 2
HUB_Z = 11
VMEM_LIMIT = 40 * 2**20
UNROLL = 4
STEPS = 4


def tap_constants():
    place = np.arange(TAPS * FRAME, dtype=np.float64) + 0.5
    shifted = (place - 2.0 * FRAME) / FRAME
    window = 0.5 - 0.5 * np.cos(place * (2.0 * math.pi / (TAPS * FRAME)))
    taps = (np.sinc(shifted) * window).reshape(TAPS, FRAME).astype(np.float32)
    return taps * np.float32(0.25)


def cos_sin(phase):
    turn = (phase + FRAME // 8) >> 9
    rest = (phase - (turn << 9)).astype(jnp.float32) * (2.0 * math.pi / FRAME)
    sq = rest * rest
    sin = rest * (1.0 + sq * (-1.0 / 6 + sq * (1.0 / 120 + sq * (-1.0 / 5040 + sq * (1.0 / 362880)))))
    cos = 1.0 + sq * (-0.5 + sq * (1.0 / 24 + sq * (-1.0 / 720 + sq * (1.0 / 40320))))
    odd = (turn & 1) == 1
    c = jnp.where(odd, sin, cos)
    s = jnp.where(odd, cos, sin)
    c = jnp.where(((turn + 1) & 2) == 2, -c, c)
    s = jnp.where((turn & 2) == 2, -s, s)
    return c, s


def taps_applied(ext, taps):
    prior = pltpu.roll(ext, 1, 0)
    early = taps[1:2] * ext + taps[0:1] * prior
    late = taps[3:4] * ext + taps[2:3] * prior
    return (late + pltpu.roll(early, 2, 0))[8:].astype(jnp.bfloat16)


def centred(samples):
    return samples.astype(jnp.float32) - 7.5


def make_table(chan_ref, table, lo, hi):
    rows = 16
    lane = lax.broadcasted_iota(jnp.int32, (rows, LANES), 1)
    scale = 1.0 / math.sqrt(FRAME)

    @pl.loop(lo, hi, unroll=2)
    def _(block):
        row = lax.broadcasted_iota(jnp.int32, (rows, LANES), 0) + block * rows
        source = ((row >> 1) & 3) * (NZ * NX) + (row >> 3) * NX + (row & 1)
        picked = jnp.where(lane == source, jnp.broadcast_to(chan_ref[...], (rows, LANES)), 0)
        chan = jnp.sum(picked.astype(jnp.float32), axis=1, keepdims=True)
        chan = jnp.broadcast_to(chan, (rows, LANES)).astype(jnp.int32)
        re, im = cos_sin((chan * lane) & (FRAME - 1))
        parts = [(re * scale, -im * scale)]
        for step in (128, 256):
            c, s = cos_sin((chan * step) & (FRAME - 1))
            parts += [(a * c + b * s, b * c - a * s) for a, b in parts]
        quarter = chan & 3
        c = jnp.where(quarter == 0, 1.0, jnp.where(quarter == 2, -1.0, 0.0))
        s = jnp.where(quarter == 1, 1.0, jnp.where(quarter == 3, -1.0, 0.0))
        parts += [(a * c + b * s, b * c - a * s) for a, b in parts]
        sign = (1 - 2 * (chan & 1)).astype(jnp.float32)
        parts += [(a * sign, b * sign) for a, b in parts]
        at = pl.multiple_of(block * rows, rows)
        for k, (a, b) in enumerate(parts):
            table[pl.ds(at, rows), k * LANES : (k + 1) * LANES] = a.astype(jnp.bfloat16)
            table[pl.ds(at + CHANS, rows), k * LANES : (k + 1) * LANES] = b.astype(jnp.bfloat16)


def channelize_kernel(
    samples, chan_hbm, taps_hbm, turned,
    raw, chan_ref, taps_ref, filtered, table, spread, mine, held, edge_out, edge_in,
    load_sem, edge_sem, zsend, zrecv, psend, precv, in_sem, plane_sem, late_sem,
):
    freq = lax.axis_index("freq")
    tm = lax.axis_index("tm")
    bl = lax.axis_index("bl")
    y, z = freq // NZ, freq % NZ
    half = y // 2

    barrier = pltpu.get_barrier_semaphore()
    partner = (freq, 1 - tm, bl)
    early = z < EARLY
    along_hub = z == HUB_Z
    plane_hub = (y == 2) & (tm == 1) & (bl == 0)
    hub = along_hub | plane_hub

    def signal(sem, device):
        pl.semaphore_signal(sem, inc=1, device_id=device, device_id_type=MESH)

    def along(t):
        return (y * NZ + t, tm, bl)

    signal(barrier, partner)

    loads = [
        pltpu.make_async_copy(samples.at[:, 56:64], raw.at[:, 56:64], load_sem.at[0]),
        pltpu.make_async_copy(chan_hbm, chan_ref, load_sem.at[5]),
        pltpu.make_async_copy(taps_hbm, taps_ref, load_sem.at[6]),
    ]
    for i in range(4):
        loads.append(pltpu.make_async_copy(samples.at[i, 0:56], raw.at[i, 0:56], load_sem.at[1 + i]))
    for copy in loads:
        copy.start()

    @pl.when(early)
    def _():
        @pl.loop(z + 1, NZ)
        def _(t):
            signal(barrier, along(t))

    @pl.when(jnp.logical_not(early | along_hub))
    def _():
        signal(barrier, along(HUB_Z))

    @pl.when(jnp.logical_not(plane_hub))
    def _():
        signal(barrier, (2 * NZ + z, 1, 0))

    contacts = jnp.where(early, z, jnp.where(along_hub, NZ - 1, EARLY))
    contacts += jnp.where(plane_hub, 32, 1)

    loads[0].wait()
    edge_copy = pltpu.make_async_remote_copy(
        edge_out, edge_in, edge_sem.at[0], edge_sem.at[1], device_id=partner, device_id_type=MESH
    )
    for f in range(TAPS - 1):
        last = [raw[i, 64 - (TAPS - 1) + f : 65 - (TAPS - 1) + f] for i in range(4)]
        edge_out[f] = centred(jnp.concatenate(last, axis=0)).astype(jnp.bfloat16)
    loads[1].wait()
    make_table(chan_ref, table, 0, 4)

    def pass_on():
        @pl.when(along_hub)
        def _():
            for t in range(EARLY, NZ):
                if t != HUB_Z:
                    signal(late_sem, along(t))

        @pl.when(plane_hub)
        def _():
            for n in range(31, 0, -1):
                signal(plane_sem, ((y + n // 8) % NY * NZ + z, (tm + n // 4) % NX, (bl + n) % 4))

    def meet():
        pl.semaphore_wait(barrier, contacts)

        @pl.when(tm == 0)
        def _():
            edge_copy.start()

        @pl.loop(0, jnp.where(early, z, EARLY))
        def _(t):
            signal(in_sem.at[z], along(t))

        pass_on()

    @pl.when(jnp.logical_not(hub))
    def _():
        meet()

    make_table(chan_ref, table, 4, 8)
    loads[2].wait()

    for i in range(4):
        loads[3 + i].wait()

        @pl.loop(0, FRAME // LANES, unroll=UNROLL)
        def _(k):
            cols = pl.ds(pl.multiple_of(k * LANES, LANES), LANES)
            filtered[i * 64 + 8 : i * 64 + 64, cols] = taps_applied(centred(raw[i, :, cols]), taps_ref[:, cols])

    @pl.when(hub)
    def _():
        meet()

    @pl.when(tm == 0)
    def _():
        edge_in[...] = jnp.zeros_like(edge_in)
        edge_copy.wait_send()

    @pl.when(tm == 1)
    def _():
        edge_copy.wait_recv()

    @pl.loop(0, FRAME // LANES, unroll=2)
    def _(k):
        cols = pl.ds(pl.multiple_of(k * LANES, LANES), LANES)
        before = [edge_in[f, :, cols].astype(jnp.float32) for f in range(TAPS - 1)]
        for i in range(4):
            past = [before[f][i : i + 1] for f in (0, 0, 0, 0, 0, 0, 1, 2)]
            ext = jnp.concatenate(past + [centred(raw[i, 0:8, cols])], axis=0)
            filtered[i * 64 : i * 64 + 8, cols] = taps_applied(ext, taps_ref[:, cols])

    spectra = lax.dot_general(
        table[...], filtered[...], (((1,), (1,)), ((), ())), preferred_element_type=jnp.float32
    )
    first = lax.broadcasted_iota(jnp.int32, (CHANS, LANES), 1) < 64
    for t in range(2):
        re = spectra[:CHANS, t * LANES : (t + 1) * LANES]
        im = spectra[CHANS:, t * LANES : (t + 1) * LANES]
        spread[pl.ds(2 * t, CHANS, stride=4), :] = jnp.where(first, re, pltpu.roll(im, 64, 1))
        spread[pl.ds(2 * t + 1, CHANS, stride=4), :] = jnp.where(first, pltpu.roll(re, 64, 1), im)
    mine[...] = spread[...].astype(jnp.bfloat16).reshape(NZ, NY * NX, 4, LANES)

    def send_along(t):
        d = (z - t + 7 + NZ) % NZ - 7
        slot = jnp.where(d > 0, 2 * d - 1, -2 * d)
        wave = sum((slot >= lo).astype(jnp.int32) for lo, _ in WAVES[1:])
        pltpu.make_async_remote_copy(
            mine.at[t], held.at[slot], zsend, zrecv.at[wave], device_id=along(t), device_id_type=MESH
        ).start()

    pltpu.make_async_copy(mine.at[z], held.at[0], zrecv.at[0]).start()

    @pl.when(early)
    def _():
        @pl.loop(0, z)
        def _(t):
            send_along(t)

        @pl.loop(z + 1, NZ)
        def _(t):
            pl.semaphore_wait(in_sem.at[t], 1)
            send_along(t)

    @pl.when(jnp.logical_not(early))
    def _():
        @pl.loop(0, EARLY)
        def _(t):
            send_along(t)

        @pl.when(jnp.logical_not(along_hub))
        def _():
            pl.semaphore_wait(late_sem, 1)

        @pl.loop(EARLY, z)
        def _(t):
            send_along(t)

        @pl.loop(z + 1, NZ)
        def _(t):
            send_along(t)

    @pl.when(jnp.logical_not(plane_hub))
    def _():
        pl.semaphore_wait(plane_sem, 1)

    for w, (lo, hi) in enumerate(WAVES):
        pltpu.make_async_copy(held.at[lo:hi], held.at[lo:hi], zrecv.at[w]).wait()
        land = turned.at[tm, y, lo:hi, bl]
        for y_to in range(NY):
            for x_to in range(NX):
                block = held.at[lo:hi, y_to * NX + x_to]
                for to in (1, 3 * half, 2):
                    here = (y_to == y) & (x_to == tm) & (to == bl)

                    @pl.when(jnp.logical_not(here))
                    def _():
                        pltpu.make_async_remote_copy(
                            block, land, psend.at[w], precv.at[w],
                            device_id=(y_to * NZ + z, x_to, to), device_id_type=MESH,
                        ).start()

                    @pl.when(here)
                    def _():
                        pltpu.make_async_copy(block, land, precv.at[w]).start()

    middle = (bl == 1) | (bl == 2)
    to_self = middle | (bl == 3 * half)
    for w, (lo, hi) in enumerate(WAVES):

        @pl.when(to_self)
        def _():
            sent = spread.at[0 : 46 * (hi - lo)]
            pltpu.make_async_copy(sent, sent, psend.at[w]).wait()

        @pl.when(jnp.logical_not(to_self))
        def _():
            sent = spread.at[0 : 48 * (hi - lo)]
            pltpu.make_async_copy(sent, sent, psend.at[w]).wait()

        @pl.when(middle)
        def _():
            got = turned.at[:, :, lo:hi]
            pltpu.make_async_copy(got, got, precv.at[w]).wait()

        @pl.when(jnp.logical_not(middle))
        def _():
            got = turned.at[:, 0:2, lo:hi]
            pltpu.make_async_copy(got, got, precv.at[w]).wait()

    sent = mine.at[0 : NZ - 1]
    pltpu.make_async_copy(sent, sent, zsend).wait()


def correlate_kernel(turned, out, made, sems):
    z = lax.axis_index("freq") % NZ
    bl = lax.axis_index("bl")

    def rows(half, first, count):
        parts = []
        for n in range(first, first + count // 16):
            d = (n % NZ - z + 7 + NZ) % NZ - 7
            slot = jnp.where(d > 0, 2 * d - 1, -2 * d)
            parts.append([turned[x, half * 2 + n // NZ, slot] for x in range(NX)])
        return [jnp.concatenate(p, axis=0) for p in zip(*parts)]

    sign = jnp.where(lax.broadcasted_iota(jnp.int32, (1, LANES), 1) < 64, 1.0, -1.0)
    cols = jnp.concatenate(rows(bl % 2, 0, 512), axis=1)
    count = 512 // STEPS
    copies = []
    for step in range(STEPS):
        halves = rows(bl // 2, step * count // 16, count)
        turned_halves = [(pltpu.roll(h.astype(jnp.float32), 64, 1) * sign).astype(jnp.bfloat16) for h in halves]
        left = jnp.concatenate([jnp.concatenate(h, axis=1) for h in (halves, turned_halves)], axis=0)
        product = lax.dot_general(left, cols, (((1,), (1,)), ((), ())), preferred_element_type=jnp.float32)
        place = slice(step * count, (step + 1) * count)
        for p in range(2):
            made[0, 0, p, place] = product[p * count : (p + 1) * count] * (1.0 / 128)
        copies.append(pltpu.make_async_copy(made.at[:, :, :, place], out.at[:, :, :, place], sems.at[step]))
        copies[-1].start()
    for copy in copies:
        copy.wait()


def on_device(samples, chan_index):
    bf16, f32 = jnp.bfloat16, jnp.float32
    hbm = pl.BlockSpec(memory_space=pltpu.MemorySpace.HBM)
    dma = pltpu.SemaphoreType.DMA
    inputs = (samples, chan_index.reshape(1, CHANS), jnp.asarray(tap_constants()))
    turned = pl.pallas_call(
        channelize_kernel,
        out_shape=jax.ShapeDtypeStruct((NX, NY, NZ, 4, 4, LANES), bf16),
        in_specs=[hbm, hbm, hbm],
        out_specs=pl.BlockSpec(memory_space=pl.ANY),
        scratch_shapes=[
            pltpu.VMEM((4, 64, FRAME), jnp.int32),
            pltpu.VMEM((1, CHANS), jnp.int32),
            pltpu.VMEM((TAPS, FRAME), f32),
            pltpu.VMEM((256, FRAME), bf16),
            pltpu.VMEM((2 * CHANS, FRAME), bf16),
            pltpu.VMEM((4 * CHANS, LANES), f32),
            pltpu.VMEM((NZ, NY * NX, 4, LANES), bf16),
            pltpu.VMEM((NZ, NY * NX, 4, LANES), bf16),
            pltpu.VMEM((TAPS - 1, 4, FRAME), bf16),
            pltpu.VMEM((TAPS - 1, 4, FRAME), bf16),
            dma((7,)),
            dma((2,)),
            dma,
            dma((len(WAVES),)),
            dma((len(WAVES),)),
            dma((len(WAVES),)),
            pltpu.SemaphoreType.REGULAR((NZ,)),
            pltpu.SemaphoreType.REGULAR,
            pltpu.SemaphoreType.REGULAR,
        ],
        compiler_params=pltpu.CompilerParams(
            collective_id=0, has_side_effects=True, vmem_limit_bytes=VMEM_LIMIT
        ),
        name="channelize",
    )(*(pltpu.with_memory_space_constraint(a, pltpu.MemorySpace.HBM) for a in inputs))
    turned = turned.reshape(NX, NY, NZ, 16, LANES)
    return pl.pallas_call(
        correlate_kernel,
        out_shape=jax.ShapeDtypeStruct((1, 1, 2, 512, 512), f32),
        in_specs=[pl.BlockSpec(memory_space=pltpu.VMEM)],
        out_specs=hbm,
        scratch_shapes=[
            pltpu.VMEM((1, 1, 2, 512, 512), f32),
            dma((STEPS,)),
        ],
        compiler_params=pltpu.CompilerParams(vmem_limit_bytes=VMEM_LIMIT),
        name="correlate",
    )(turned)


def solution(mesh):
    placed = (P(("freq", "bl"), "tm", None), P())
    return jax.shard_map(
        on_device,
        mesh=mesh,
        in_specs=placed,
        out_specs=P(("freq", "tm"), "bl", None, None, None),
        check_vma=False,
    )
```

time: 33.9 us -> 33 us (0.973)
  Pallas kernels: 33.7 us -> 32.6 us
    pallas_call x1, Pallas kernels: 2.67 us -> 1.66 us  [on_device(): pl.pallas_call(correlate_kernel, out_shape=jax.ShapeDtypeStruct((1, 1, 2,...]
where the time goes in v3:
time: 33 us; the launch traced here: 32.6 us
  Pallas kernels  32.6 us (99%)
    pallas_call x1, Pallas kernels, on_device(): pl.pallas_call(channelize_kernel, out_shape=jax.ShapeDtypeStruct((NX, NY,...  31 us
    pallas_call x1, Pallas kernels, on_device(): pl.pallas_call(correlate_kernel, out_shape=jax.ShapeDtypeStruct((1, 1, 2,...  1.66 us

profile of v3, /device:TPU:1, one launch (start us, length us, event | category | flops | bytes accessed | tf_op | source)
XLA Modules:
  0.0 32.6 jit_solution(17561219981728230428)
XLA Ops:
  0.0 31.0 %channelize.1 = bf16[2,4,16,4,4,128]{5,4,3,2,1,0:T(4,128)(2,1)S(1)} custom-call(s32[4,64,2048]{2,1,0:T(8,128)} %samples.1, s32[1,128]{1,0:T(1,128)} %bitcast.3, f32[4,2048]{1,0:T(4,128)} %constant.2.clone.taps_hbm), custom_call_target="tpu_custom_call" | custom-call | tf_op jit(solution)/shard_map/channelize/pallas_call | solution.py:350
  31.0 1.7 %correlate.1 = f32[1,1,2,512,512]{4,3,2,1,0:T(8,128)} custom-call(bf16[2,4,16,16,128]{4,3,2,1,0:T(8,128)(2,1)S(1)} %bitcast.2), custom_call_target="tpu_custom_call" | custom-call | tf_op jit(solution)/shard_map/correlate/pallas_call | solution.py:382

commit v4 on v3

--- a/solution.py
+++ b/solution.py
@@ -146,7 +146,11 @@
         last = [raw[i, 64 - (TAPS - 1) + f : 65 - (TAPS - 1) + f] for i in range(4)]
         edge_out[f] = centred(jnp.concatenate(last, axis=0)).astype(jnp.bfloat16)
     loads[1].wait()
-    make_table(chan_ref, table, 0, 4)
+    make_table(chan_ref, table, 0, 6)
+
+    def plane_in():
+        for n in range(31, 0, -1):
+            signal(plane_sem, ((y + n // 8) % NY * NZ + z, (tm + n // 4) % NX, (bl + n) % 4))
 
     def pass_on():
         @pl.when(along_hub)
@@ -155,10 +159,9 @@
                 if t != HUB_Z:
                     signal(late_sem, along(t))
 
-        @pl.when(plane_hub)
-        def _():
-            for n in range(31, 0, -1):
-                signal(plane_sem, ((y + n // 8) % NY * NZ + z, (tm + n // 4) % NX, (bl + n) % 4))
+        @pl.when(plane_hub & early)
+        def _():
+            plane_in()
 
     def meet():
         pl.semaphore_wait(barrier, contacts)
@@ -177,7 +180,7 @@
     def _():
         meet()
 
-    make_table(chan_ref, table, 4, 8)
+    make_table(chan_ref, table, 6, 8)
     loads[2].wait()
 
     for i in range(4):
@@ -248,6 +251,10 @@
         def _(t):
             send_along(t)
 
+        @pl.when(plane_hub)
+        def _():
+            plane_in()
+
         @pl.when(jnp.logical_not(along_hub))
         def _():
             pl.semaphore_wait(late_sem, 1)
@@ -267,7 +274,7 @@
     for w, (lo, hi) in enumerate(WAVES):
         pltpu.make_async_copy(held.at[lo:hi], held.at[lo:hi], zrecv.at[w]).wait()
         land = turned.at[tm, y, lo:hi, bl]
-        for y_to in range(NY):
+        for y_to in ((y + 2) % NY, (y + 1) % NY, (y + 3) % NY, y):
             for x_to in range(NX):
                 block = held.at[lo:hi, y_to * NX + x_to]
                 for to in (1, 3 * half, 2):

time: 33 us -> 32.8 us (level)
  no operation moved by 1% of the time
where the time goes in v4:
time: 32.8 us; the launch traced here: 32.7 us
  Pallas kernels  32.6 us (99%)
    pallas_call x1, Pallas kernels, on_device(): pl.pallas_call(channelize_kernel, out_shape=jax.ShapeDtypeStruct((NX, NY,...  31 us
    pallas_call x1, Pallas kernels, on_device(): pl.pallas_call(correlate_kernel, out_shape=jax.ShapeDtypeStruct((1, 1, 2,...  1.66 us

profile of v4, /device:TPU:1, one launch (start us, length us, event | category | flops | bytes accessed | tf_op | source)
XLA Modules:
  0.0 32.7 jit_solution(17442035645056028018)
XLA Ops:
  0.0 31.0 %channelize.1 = bf16[2,4,16,4,4,128]{5,4,3,2,1,0:T(4,128)(2,1)S(1)} custom-call(s32[4,64,2048]{2,1,0:T(8,128)} %samples.1, s32[1,128]{1,0:T(1,128)} %bitcast.3, f32[4,2048]{1,0:T(4,128)} %constant.2.clone.taps_hbm), custom_call_target="tpu_custom_call" | custom-call | tf_op jit(solution)/shard_map/channelize/pallas_call | solution.py:357
  31.0 1.7 %correlate.1 = f32[1,1,2,512,512]{4,3,2,1,0:T(8,128)} custom-call(bf16[2,4,16,16,128]{4,3,2,1,0:T(8,128)(2,1)S(1)} %bitcast.2), custom_call_target="tpu_custom_call" | custom-call | tf_op jit(solution)/shard_map/correlate/pallas_call | solution.py:389

commit v5 on v4

--- a/solution.py
+++ b/solution.py
@@ -15,7 +15,7 @@
 LANES = 128
 MESH = pl.DeviceIdType.MESH
 OFFSETS = (0, 1, -1, 2, -2, 3, -3, 4, -4, 5, -5, 6, -6, 7, -7, 8)
-WAVES = ((0, 7), (7, 11), (11, 15), (15, 16))
+WAVES = ((0, 9), (9, 15), (15, 16))
 EARLY = NZ // 2
 HUB_Z = 11
 VMEM_LIMIT = 40 * 2**20

time: 32.8 us -> 32.8 us (level)
  no operation moved by 1% of the time
where the time goes in v5:
time: 32.8 us; the launch traced here: 32.6 us
  Pallas kernels  32.6 us (99%)
    pallas_call x1, Pallas kernels, on_device(): pl.pallas_call(channelize_kernel, out_shape=jax.ShapeDtypeStruct((NX, NY,...  30.9 us
    pallas_call x1, Pallas kernels, on_device(): pl.pallas_call(correlate_kernel, out_shape=jax.ShapeDtypeStruct((1, 1, 2,...  1.68 us

profile of v5, /device:TPU:1, one launch (start us, length us, event | category | flops | bytes accessed | tf_op | source)
XLA Modules:
  0.0 32.6 jit_solution(13231526384617609575)
XLA Ops:
  0.0 30.9 %channelize.1 = bf16[2,4,16,4,4,128]{5,4,3,2,1,0:T(4,128)(2,1)S(1)} custom-call(s32[4,64,2048]{2,1,0:T(8,128)} %samples.1, s32[1,128]{1,0:T(1,128)} %bitcast.3, f32[4,2048]{1,0:T(4,128)} %constant.2.clone.taps_hbm), custom_call_target="tpu_custom_call" | custom-call | tf_op jit(solution)/shard_map/channelize/pallas_call | solution.py:357
  31.0 1.7 %correlate.1 = f32[1,1,2,512,512]{4,3,2,1,0:T(8,128)} custom-call(bf16[2,4,16,16,128]{4,3,2,1,0:T(8,128)(2,1)S(1)} %bitcast.2), custom_call_target="tpu_custom_call" | custom-call | tf_op jit(solution)/shard_map/correlate/pallas_call | solution.py:389
